TPU v7x, 512 devices: a whole 4x8x8 slice. The times are simulated.
512 devices in a mesh: strike: 64 (over y_hi, z, x), normal: 8 (over y_lo, core).
Axes of the slice: x: 4, y: 8 (y_hi: 2, y_lo: 4; y = y_hi * 4 + y_lo), z: 8, core: 2. Of those that a mesh axis runs over, the one named last changes fastest.
Arguments:
- displacement: float32 [3, 2048, 64, 128], P(None, 'strike', 'normal'), may hold values from -6 to 6
- velocity: float32 [3, 2048, 64, 128], P(None, 'strike', 'normal'), may hold values from -6 to 6
- stiffness: float32 [2048, 64, 128], P('strike', 'normal'), may hold values from 0.4 to 1.3
- yield_flags: int32 [512, 64, 32], P('strike', 'normal'), may hold values from 0 to 1
- contact: int32 [2, 2048, 128], P(None, 'strike'), may hold values 0 or 1
- history: bfloat16 [2, 8, 2, 3, 128, 2048], P(None, None, None, None, 'strike'), may hold values from -6 to 6
- kernel: float32 [2, 8, 3, 2048], replicated, may hold values from -1.8 to 1.8
Outputs:
- final_displacement: float32 [3, 2048, 64, 128], P(None, 'strike', 'normal')
- final_velocity: float32 [3, 2048, 64, 128], P(None, 'strike', 'normal')
All inputs are finite; a program needn't handle non-finite values. No bound on the sum of `contact` on one device may be relied on, other than what follows from the above.
Results may differ from a plain program's by a relative error of at most 0.001.
Values may be sent and summed in bfloat16 or wider, within the bound.
A program may use at most 64 MiB of HBM per device.

v0:
```python
import functools
import math

import jax
import jax.numpy as jnp
import numpy as np
from jax import lax
from jax.experimental import pallas as pl
from jax.experimental.pallas import tpu as pltpu
from jax.sharding import PartitionSpec as P

MESH = pl.DeviceIdType.MESH
SUB = 3
time_step = 0.5

YH, NZ, NX = 2, 8, 4
GROUP = YH * NX
SLABS = YH * NZ * NX
OWN = 32
NS = SLABS * OWN
N1, N2 = 128, 16
F32, BF16 = jnp.float32, jnp.bfloat16


def tables():
    z = np.arange(NZ)[:, None]
    b = np.arange(GROUP)[None, :]
    slab_zb = ((b // NX) * (NZ * NX) + z * NX + b % NX).reshape(-1)
    slab_bz = ((b // NX) * (NZ * NX) + z * NX + b % NX).T.reshape(-1)
    k1 = np.arange(N1)
    n2 = np.arange(N2)
    t = np.arange(N2)
    first = np.concatenate([2 * slab_bz, 2 * slab_bz + 1])
    angle = 2 * np.pi * (np.outer(first, k1) % N1) / N1
    forward = np.concatenate([np.cos(angle), -np.sin(angle)], axis=1)
    twist = 2 * np.pi * np.outer(n2, k1) / NS / 1.0
    norm = 1.0 / math.sqrt(NS)
    twiddle = norm * np.stack([np.tile(np.cos(twist), (8, 1)), np.tile(-np.sin(twist), (8, 1))])
    small = 2 * np.pi * (np.outer(t, n2) % N2) / N2
    co, si = np.cos(small), np.sin(small)
    inner = np.zeros((2, 3, 2, N2, 2, 2, 4, N2))
    outer = np.zeros((2, 2, 4, N2, 2, 3, 2, N2))
    for c in range(3):
        for dd in range(2):
            inner[0, c, dd, :, 0, dd, c, :] = co
            inner[0, c, dd, :, 1, dd, c, :] = si
            inner[1, c, dd, :, 0, dd, c, :] = -si
            inner[1, c, dd, :, 1, dd, c, :] = co
            outer[0, dd, c, :, 0, c, dd, :] = co.T
            outer[0, dd, c, :, 1, c, dd, :] = -si.T
            outer[1, dd, c, :, 0, c, dd, :] = si.T
            outer[1, dd, c, :, 1, c, dd, :] = co.T
    inner = inner.reshape(192, 256)
    outer = outer.reshape(256, 192)
    last = np.concatenate([2 * slab_zb - 1 + r for r in range(4)]) % N1
    angle = 2 * np.pi * (np.outer(last, k1) % N1) / N1
    inverse = np.concatenate([np.cos(angle), -np.sin(angle)], axis=1)
    dips = np.arange(128)[None, :]
    pack = np.stack([dips == 2 * slab_zb[:, None] + dd for dd in range(2)])
    unpack = np.stack([dips == 2 * slab_bz[:, None] + dd for dd in range(2)])
    widen = np.arange(32)[:, None] == dips // 4
    bf = [forward, inner, outer, inverse, pack, unpack, widen]
    return [jnp.asarray(a.astype(np.float32), dtype=BF16) for a in bf] + [
        jnp.asarray(twiddle.astype(np.float32))
    ]


def mm(a, b):
    return jnp.dot(a.astype(BF16), b.astype(BF16), preferred_element_type=F32)


def mm_nt(a, b):
    return lax.dot_general(
        a.astype(BF16), b.astype(BF16), (((1,), (1,)), ((), ())), preferred_element_type=F32
    )


def dip_sides(x):
    axis = x.ndim - 1
    lane = lax.broadcasted_iota(jnp.int32, x.shape, axis)
    below = jnp.where(lane == 0, 0.0, pltpu.roll(x, 1, axis))
    above = jnp.where(lane == 127, 0.0, pltpu.roll(x, 127, axis))
    return below + above


def kernel(
    u_in, v_in, stiff_in, flags_in, contact_in, past_in, newest_in,
    forward_in, inner_in, outer_in, inverse_in, pack_in, unpack_in, widen_in, twiddle_in,
    u_out, v_out,
    us0, us1, us2, uf, vs, stiff, flags, mods, contacts, past, newest,
    forward, inner, outer, inverse, pack, unpack, widen, twiddle,
    faces, sides, p1, g1, r1, p2, g2, q2, force, mod2,
    in_sem, out_sem, self_sem, halo_s, halo_r, aux_s, aux_r, a2a_s, a2a_r,
):
    s = lax.axis_index("strike")
    m = lax.axis_index("normal")
    my_z = (s // NX) % NZ
    my_b = (s // (NX * NZ)) * NX + s % NX
    low, high = m == 0, m == 7
    plane = jnp.logical_or(low, high)
    left, right = (s + SLABS - 1) % SLABS, (s + 1) % SLABS
    mine_b_base = (my_b // NX) * (NZ * NX) + my_b % NX

    def z_peer(i):
        z = (my_z + i) % NZ
        return z, mine_b_base + z * NX

    def b_peer(i):
        b = (my_b + i) % GROUP
        return b, (b // NX) * (NZ * NX) + my_z * NX + b % NX

    barrier = pltpu.get_barrier_semaphore()

    def greet(**where):
        pl.semaphore_signal(barrier, inc=1, device_id=where, device_id_type=MESH)

    greet(strike=left)
    greet(strike=right)

    @pl.when(jnp.logical_not(low))
    def _():
        greet(normal=m - 1)

    @pl.when(jnp.logical_not(high))
    def _():
        greet(normal=m + 1)

    @pl.when(plane)
    def _():
        for i in range(1, NZ):
            greet(strike=z_peer(i)[1])
        for i in range(1, GROUP):
            greet(strike=b_peer(i)[1])

    loads = [
        pltpu.make_async_copy(u_in, us0.at[:, pl.ds(1, OWN)], in_sem.at[0]),
        pltpu.make_async_copy(pack_in, pack, in_sem.at[1]),
        pltpu.make_async_copy(flags_in, flags, in_sem.at[2]),
        pltpu.make_async_copy(stiff_in, stiff, in_sem.at[3]),
        pltpu.make_async_copy(widen_in, widen, in_sem.at[4]),
        pltpu.make_async_copy(contact_in, contacts.at[pl.ds(8, OWN)], in_sem.at[5]),
        pltpu.make_async_copy(v_in, vs, in_sem.at[6]),
        pltpu.make_async_copy(forward_in, forward, in_sem.at[7]),
        pltpu.make_async_copy(inner_in, inner, in_sem.at[8]),
        pltpu.make_async_copy(outer_in, outer, in_sem.at[9]),
        pltpu.make_async_copy(inverse_in, inverse, in_sem.at[10]),
        pltpu.make_async_copy(unpack_in, unpack, in_sem.at[11]),
        pltpu.make_async_copy(twiddle_in, twiddle, in_sem.at[12]),
        pltpu.make_async_copy(past_in, past, in_sem.at[13]),
        pltpu.make_async_copy(newest_in, newest, in_sem.at[14]),
    ]
    for load in loads:
        load.start()

    def strike_copies(i, src):
        return [
            pltpu.make_async_remote_copy(
                src.at[:, OWN], src.at[:, 0], halo_s.at[i, 0], halo_r.at[i, 0],
                device_id={"strike": right}, device_id_type=MESH,
            ),
            pltpu.make_async_remote_copy(
                src.at[:, 1], src.at[:, OWN + 1], halo_s.at[i, 1], halo_r.at[i, 1],
                device_id={"strike": left}, device_id_type=MESH,
            ),
        ]

    def up_copy(i):
        return pltpu.make_async_remote_copy(
            faces.at[i, 1], sides.at[i, 0], halo_s.at[i, 2], halo_r.at[i, 2],
            device_id={"normal": m + 1}, device_id_type=MESH,
        )

    def down_copy(i):
        return pltpu.make_async_remote_copy(
            faces.at[i, 0], sides.at[i, 1], halo_s.at[i, 3], halo_r.at[i, 3],
            device_id={"normal": m - 1}, device_id_type=MESH,
        )

    def start_halo(i, src):
        for copy in strike_copies(i, src):
            copy.start()

        @pl.when(jnp.logical_not(high))
        def _():
            up_copy(i).start()

        @pl.when(jnp.logical_not(low))
        def _():
            down_copy(i).start()

    def wait_halo(i, src):
        for copy in strike_copies(i, src):
            copy.wait_recv()

        @pl.when(jnp.logical_not(low))
        def _():
            up_copy(i).wait_recv()

        @pl.when(jnp.logical_not(high))
        def _():
            down_copy(i).wait_recv()

    def finish_halo(i, src):
        for copy in strike_copies(i, src):
            copy.wait_send()

        @pl.when(jnp.logical_not(high))
        def _():
            up_copy(i).wait_send()

        @pl.when(jnp.logical_not(low))
        def _():
            down_copy(i).wait_send()

    def set_faces(i, src):
        faces[i, 0] = src[:, 1 : OWN + 1, 0, :]
        faces[i, 1] = src[:, 1 : OWN + 1, 7, :]

    aux = [
        pltpu.make_async_remote_copy(
            mods.at[OWN], mods.at[0], aux_s.at[0], aux_r.at[0],
            device_id={"strike": right}, device_id_type=MESH,
        ),
        pltpu.make_async_remote_copy(
            mods.at[1], mods.at[OWN + 1], aux_s.at[1], aux_r.at[1],
            device_id={"strike": left}, device_id_type=MESH,
        ),
        pltpu.make_async_remote_copy(
            contacts.at[pl.ds(OWN, 8)], contacts.at[pl.ds(0, 8)], aux_s.at[2], aux_r.at[2],
            device_id={"strike": right}, device_id_type=MESH,
        ),
        pltpu.make_async_remote_copy(
            contacts.at[pl.ds(8, 8)], contacts.at[pl.ds(OWN + 8, 8)], aux_s.at[3], aux_r.at[3],
            device_id={"strike": left}, device_id_type=MESH,
        ),
    ]

    def z_copies(k, src, dst):
        copies = []
        for i in range(1, NZ):
            z, who = z_peer(i)
            copies.append(
                pltpu.make_async_remote_copy(
                    src.at[z], dst.at[my_z], a2a_s.at[k, i], a2a_r.at[k, i],
                    device_id={"strike": who}, device_id_type=MESH,
                )
            )
        return copies, pltpu.make_async_copy(src.at[my_z], dst.at[my_z], self_sem.at[k])

    def b_copies(k, src, dst):
        copies = []
        for i in range(1, GROUP):
            b, who = b_peer(i)
            copies.append(
                pltpu.make_async_remote_copy(
                    src.at[:, b], dst.at[my_b], a2a_s.at[k, i], a2a_r.at[k, i],
                    device_id={"strike": who}, device_id_type=MESH,
                )
            )
        return copies, pltpu.make_async_copy(src.at[:, my_b], dst.at[my_b], self_sem.at[k])

    def launch(stage):
        for copy in stage[0]:
            copy.start()
        stage[1].start()

    def land(stage):
        for copy in stage[0]:
            copy.wait_recv()
        stage[1].wait()

    def drain(stage):
        for copy in stage[0]:
            copy.wait_send()

    stages = [z_copies(0, p1, g1), b_copies(1, g1, r1), z_copies(2, p2, g2), b_copies(3, g2, q2)]

    loads[0].wait()
    set_faces(0, us0)
    loads[1].wait()

    @pl.when(plane)
    def _():
        for jh in range(2):
            rows = []
            for c in range(3):
                part = pl.ds(16 * jh, 16)
                rows.append(jnp.where(high, faces[0, 1, c, part], faces[0, 0, c, part]))
            rows.append(jnp.zeros((16, 128), F32))
            block = jnp.concatenate(rows, axis=0)
            halves = [mm_nt(pack[dd], block) for dd in range(2)]
            p1[:, :, jh, :] = jnp.concatenate(halves, axis=1).reshape(NZ, GROUP, 128)

    @pl.when(low)
    def _():
        for i in range(SUB):
            sides[i, 0] = jnp.zeros((3, OWN, 128), F32)

    @pl.when(high)
    def _():
        for i in range(SUB):
            sides[i, 1] = jnp.zeros((3, OWN, 128), F32)

    loads[2].wait()
    loads[3].wait()
    loads[4].wait()
    marks = mm(flags[...].reshape(64, 32).astype(F32), widen[...]).reshape(8, 1, 8, 128)
    mods[1 : OWN + 1] = (stiff[...].reshape(8, 4, 8, 128) * (1.0 - 0.5 * marks)).reshape(OWN, 8, 128)
    loads[5].wait()

    @pl.when(plane)
    def _():
        pl.semaphore_wait(barrier, 3 + NZ - 1 + GROUP - 1)
        launch(stages[0])

    @pl.when(jnp.logical_not(plane))
    def _():
        pl.semaphore_wait(barrier, 4)

    start_halo(0, us0)
    for copy in aux:
        copy.start()

    def substep(i, src, dst, offset):
        for c in range(3):
            here = src[c, 1 : OWN + 1]
            layer = lax.broadcasted_iota(jnp.int32, here.shape, 1)
            below = jnp.where(layer == 0, sides[i, 0, c][:, None, :], pltpu.roll(here, 1, 1))
            above = jnp.where(layer == 7, sides[i, 1, c][:, None, :], pltpu.roll(here, 7, 1))
            lap = (
                src[c, 2 : OWN + 2] + src[c, 0:OWN] + (above + below) + dip_sides(here) - 6.0 * here
            )
            speed = vs[c] + time_step * (mods[1 : OWN + 1] * lap)
            vs[c] = speed
            dst[c, offset : offset + OWN] = here + time_step * speed

    @pl.when(plane)
    def _():
        land(stages[0])
        launch(stages[1])

    loads[6].wait()
    wait_halo(0, us0)
    substep(0, us0, us1, 1)
    set_faces(1, us1)
    start_halo(1, us1)

    for load in loads[7:]:
        load.wait()

    @pl.when(plane)
    def _():
        land(stages[1])
        got = jnp.concatenate([r1[:, :, jh, :].reshape(SLABS, 128) for jh in range(2)], axis=0)
        y = mm(got.T, forward[...])
        re, im = y[:, :128], y[:, 128:]
        tr, ti = twiddle[0], twiddle[1]
        turned = jnp.concatenate([re * tr - im * ti, re * ti + im * tr], axis=0)
        modes = mm(inner[...], turned)
        modal_force = newest[...] * modes + past[...]
        back = mm(outer[...], modal_force)
        re, im = back[:128], back[128:]
        turned = jnp.concatenate([re * tr + im * ti, im * tr - re * ti], axis=1)
        pulled = mm_nt(inverse[...], turned)
        for r in range(4):
            p2[:, :, r, :] = pulled[64 * r : 64 * r + 64].reshape(NZ, GROUP, 128)
        launch(stages[2])

    wait_halo(1, us1)
    substep(1, us1, us2, 1)
    set_faces(2, us2)
    start_halo(2, us2)

    @pl.when(plane)
    def _():
        land(stages[2])
        launch(stages[3])

    wait_halo(2, us2)
    substep(2, us2, uf, 0)
    for copy in aux:
        copy.wait_recv()

    @pl.when(plane)
    def _():
        mod2[...] = jnp.zeros_like(mod2)
        for k in range(3):
            mod2[k, 7:41] = jnp.where(high, mods[:, 7 - k, :], mods[:, k, :])
        land(stages[3])
        pieces = []
        for r in range(4):
            turned = q2[:, :, r, :].reshape(SLABS, 128).T
            pieces.append(mm(turned[:64], unpack[0]) + mm(turned[64:], unpack[1]))

        def lap2(x):
            return pltpu.roll(x, 1, 0) + pltpu.roll(x, 47, 0) + dip_sides(x) - 6.0 * x

        half = time_step
        for c in range(3):
            a = 16 * c
            load = contacts[...] * jnp.concatenate(
                [pieces[0][a + 8 : a + 16], pieces[1][a : a + 16],
                 pieces[2][a : a + 16], pieces[3][a : a + 8]],
                axis=0,
            )
            v0 = half * load
            u0 = half * v0
            v0, v1 = v0 + half * (mod2[0] * lap2(u0) + load), half * (mod2[1] * u0)
            u0, u1 = u0 + half * v0, half * v1
            v0, v1, v2 = (
                v0 + half * (mod2[0] * (lap2(u0) + u1) + load),
                v1 + half * (mod2[1] * (lap2(u1) + u0)),
                half * (mod2[2] * u1),
            )
            u0, u1, u2 = u0 + half * v0, u1 + half * v1, half * v2
            force[c, 0] = u0[8:40]
            force[c, 1] = u1[8:40]
            force[c, 2] = u2[8:40]
            force[c, 3] = v0[8:40]
            force[c, 4] = v1[8:40]
            force[c, 5] = v2[8:40]

        @pl.when(low)
        def _():
            for k in range(3):
                uf[:, :, k, :] = uf[:, :, k, :] + force[:, k]
                vs[:, :, k, :] = vs[:, :, k, :] + force[:, 3 + k]

        @pl.when(high)
        def _():
            for k in range(3):
                uf[:, :, 7 - k, :] = uf[:, :, 7 - k, :] + force[:, k]
                vs[:, :, 7 - k, :] = vs[:, :, 7 - k, :] + force[:, 3 + k]

    stores = [
        pltpu.make_async_copy(uf, u_out, out_sem.at[0]),
        pltpu.make_async_copy(vs, v_out, out_sem.at[1]),
    ]
    for store in stores:
        store.start()
    for i, src in enumerate((us0, us1, us2)):
        finish_halo(i, src)
    for copy in aux:
        copy.wait_send()

    @pl.when(plane)
    def _():
        for stage in stages:
            drain(stage)

    for store in stores:
        store.wait()


def body(displacement, velocity, stiffness, yield_flags, contact, history, kern):
    face = (lax.axis_index("normal") == lax.axis_size("normal") - 1).astype(jnp.int32)
    own_history = lax.dynamic_index_in_dim(history, face, 0, keepdims=False)
    own_kernel = lax.dynamic_index_in_dim(kern, face, 0, keepdims=False)
    touching = lax.dynamic_index_in_dim(contact, face, 0, keepdims=False).astype(F32)
    past = jnp.sum(own_kernel[1:, None, :, None, :] * own_history[:-1].astype(F32), axis=0)
    past = past.reshape(192, 128)
    newest = jnp.broadcast_to(own_kernel[0][None, :, None, :], (2, 3, 2, NS)).reshape(192, 128)
    any_space = pl.BlockSpec(memory_space=pl.ANY)
    dma, vmem = pltpu.SemaphoreType.DMA, pltpu.VMEM
    scratch = [
        vmem((3, OWN + 2, 8, 128), F32),
        vmem((3, OWN + 2, 8, 128), F32),
        vmem((3, OWN + 2, 8, 128), F32),
        vmem((3, OWN, 8, 128), F32),
        vmem((3, OWN, 8, 128), F32),
        vmem((OWN, 8, 128), F32),
        vmem((8, 8, 32), jnp.int32),
        vmem((OWN + 2, 8, 128), F32),
        vmem((OWN + 16, 128), F32),
        vmem((192, 128), F32),
        vmem((192, 128), F32),
        vmem((128, 256), BF16),
        vmem((192, 256), BF16),
        vmem((256, 192), BF16),
        vmem((256, 256), BF16),
        vmem((2, 64, 128), BF16),
        vmem((2, 64, 128), BF16),
        vmem((32, 128), BF16),
        vmem((2, 128, 128), F32),
        vmem((SUB, 2, 3, OWN, 128), F32),
        vmem((SUB, 2, 3, OWN, 128), F32),
        vmem((NZ, GROUP, 2, 128), F32),
        vmem((NZ, GROUP, 2, 128), F32),
        vmem((GROUP, NZ, 2, 128), F32),
        vmem((NZ, GROUP, 4, 128), F32),
        vmem((NZ, GROUP, 4, 128), F32),
        vmem((GROUP, NZ, 4, 128), F32),
        vmem((3, 6, OWN, 128), F32),
        vmem((3, OWN + 16, 128), F32),
        dma((15,)),
        dma((2,)),
        dma((4,)),
        dma((SUB, 4)),
        dma((SUB, 4)),
        dma((4,)),
        dma((4,)),
        dma((4, 8)),
        dma((4, 8)),
    ]
    out = jax.ShapeDtypeStruct(displacement.shape, F32)
    return pl.pallas_call(
        kernel,
        out_shape=(out, out),
        in_specs=[any_space] * 15,
        out_specs=(any_space, any_space),
        scratch_shapes=scratch,
        compiler_params=pltpu.CompilerParams(collective_id=0, has_side_effects=True),
        name="slab_step",
    )(displacement, velocity, stiffness, yield_flags, touching, past, newest, *tables())


def solution(mesh):
    return jax.shard_map(
        body,
        mesh=mesh,
        in_specs=(
            P(None, "strike", "normal", None),
            P(None, "strike", "normal", None),
            P("strike", "normal", None),
            P("strike", "normal", None),
            P(None, "strike", None),
            P(None, None, None, None, "strike", None),
            P(),
        ),
        out_specs=(P(None, "strike", "normal", None), P(None, "strike", "normal", None)),
        check_vma=False,
    )
```

profile of v0, /device:TPU:2, one launch (start us, length us, event | category | flops | bytes accessed | tf_op | source)
XLA Modules:
  0.0 50.0 jit_solution(10365479715073498988)
XLA Ops:
  0.6 0.0 copy-start
  0.7 1.4 %convert_bitcast_fusion.contact_in = f32[32,128]{1,0:T(8,128)} fusion(s32[2,32,128]{2,1,0:T(8,128)} %param.19, s32[]{:T(128)S(6)} %select_n.8), kind=kLoop, calls=%fused_computation.5 | loop fusion | flops 4096 | bytes 32772 | tf_op jit(solution)/shard_map/convert_element_type | solution.py:459
  2.0 0.0 copy-done
  2.1 0.7 %reshape.21.newest_in = f32[192,128]{1,0:T(8,128)} reshape(f32[2,3,2,2048]{3,2,1,0:T(2,128)S(1)} %broadcast_in_dim.9) | data formatting | bytes 196608 | tf_op jit(solution)/shard_map/reshape | solution.py:462
  2.8 0.1 copy.18
  3.0 1.4 %fusion = f32[2,3,2,2048]{3,2,1,0:T(2,128)S(1)} fusion(bf16[2,8,2,3,2,2048]{5,4,3,2,1,0:T(2,128)(2,1)} %param.20, s32[]{:T(128)S(6)} %select_n.8, f32[7,3,2048]{2,1,0:T(4,128)S(1)} %copy.18), kind=kLoop, calls=%fused_computation.1 | loop fusion | flops 491520 | bytes 614404 | tf_op jit(solution)/shard_map/reduce_sum | solution.py:460
  4.4 0.7 %reshape.20.past_in = f32[192,128]{1,0:T(8,128)} reshape(f32[2,3,2,2048]{3,2,1,0:T(2,128)S(1)} %fusion) | data formatting | bytes 196608 | tf_op jit(solution)/shard_map/reshape | solution.py:461
  5.1 42.3 %slab_step.1 = (f32[3,32,8,128]{3,2,1,0:T(8,128)}, f32[3,32,8,128]{3,2,1,0:T(8,128)}) custom-call(f32[3,32,8,128]{3,2,1,0:T(8,128)} %u_in.1, f32[3,32,8,128]{3,2,1,0:T(8,128)} %v_in.1, f32[32,8,128]{2,1,0:T(8,128)} %stiff_in.1, s32[8,8,32]{2,1,0:T(8,128)} %flags_in.1, f32[32,128]{1,0:T(8,128)} %convert_bitcast_fusion.contact_in, ...), custom_call_target="tpu_custom_call" | custom-call | tf_op jit(solution)/shard_map/slab_step/pallas_call | solution.py:506
  47.4 0.0 copy-start.1
  47.5 1.8 %copy.24 = f32[3,32,8,128]{3,2,1,0:T(8,128)} copy(f32[3,32,8,128]{3,2,1,0:T(8,128)} %get-tuple-element.4) | data formatting | bytes 786432
  49.3 0.0 copy-done.1
  49.3 0.7 %copy.25 = f32[3,32,8,128]{3,2,1,0:T(8,128)} copy(f32[3,32,8,128]{3,2,1,0:T(8,128)S(1)} %copy-done.1) | data formatting | bytes 786432
  (4 shorter events, 0.1 us)
Async XLA Ops:
  0.6 1.4 %copy-start = (f32[2,8,3,2048]{3,1,2,0:T(8,128)S(1)}, f32[2,8,3,2048]{3,1,2,0:T(8,128)}, u32[]{:S(2)}) copy-start(f32[2,8,3,2048]{3,1,2,0:T(8,128)} %param.21) | copy-start | bytes 1179652
  47.4 1.8 %copy-start.1 = (f32[3,32,8,128]{3,2,1,0:T(8,128)S(1)}, f32[3,32,8,128]{3,2,1,0:T(8,128)}, u32[]{:S(2)}) copy-start(f32[3,32,8,128]{3,2,1,0:T(8,128)} %get-tuple-element.5) | copy-start | bytes 1179652
where the time goes:
time: 50.2 us; the launch traced here: 50 us
  Pallas kernels  42.3 us (84%)
  local copies, waits for them, and re-layouts  4.21 us (8%)
  other arithmetic  2.78 us (6%)
  between operations  0.7 us (1%)
    pallas_call x1, Pallas kernels, body(): pl.pallas_call(kernel, out_shape=(out, out), in_specs=[any_space] * 15, o...  42.3 us
    unnamed x7, local copies, waits for them, and re-layouts  2.59 us
    reduce_sum x1, other arithmetic, body(): jnp.sum(own_kernel[1:, None, :, None, :] * own_history[:-1].astype(F32),...  1.42 us
    convert_element_type x1, other arithmetic, body(): lax.dynamic_index_in_dim(contact, face, 0, keepdims=False).astype(F32)  1.37 us

commit v1 on v0

--- a/solution.py
+++ b/solution.py
@@ -84,13 +84,13 @@
 
 
 def kernel(
-    u_in, v_in, stiff_in, flags_in, contact_in, past_in, newest_in,
+    u_in, v_in, stiff_in, flags_in, contact_in, history_in, kern_in,
     forward_in, inner_in, outer_in, inverse_in, pack_in, unpack_in, widen_in, twiddle_in,
-    u_out, v_out,
-    us0, us1, us2, uf, vs, stiff, flags, mods, contacts, past, newest,
+    uf, vs, force,
+    us0, us1, us2, stiff, flags, mods, marked, contacts, history, kern, past,
     forward, inner, outer, inverse, pack, unpack, widen, twiddle,
-    faces, sides, p1, g1, r1, p2, g2, q2, force, mod2,
-    in_sem, out_sem, self_sem, halo_s, halo_r, aux_s, aux_r, a2a_s, a2a_r,
+    faces, sides, p1, g1, r1, p2, g2, q2, mod2,
+    in_sem, past_sem, self_sem, halo_s, halo_r, aux_s, aux_r, a2a_s, a2a_r,
 ):
     s = lax.axis_index("strike")
     m = lax.axis_index("normal")
@@ -98,6 +98,7 @@
     my_b = (s // (NX * NZ)) * NX + s % NX
     low, high = m == 0, m == 7
     plane = jnp.logical_or(low, high)
+    face = m // 7
     left, right = (s + SLABS - 1) % SLABS, (s + 1) % SLABS
     mine_b_base = (my_b // NX) * (NZ * NX) + my_b % NX
 
@@ -138,7 +139,7 @@
         pltpu.make_async_copy(flags_in, flags, in_sem.at[2]),
         pltpu.make_async_copy(stiff_in, stiff, in_sem.at[3]),
         pltpu.make_async_copy(widen_in, widen, in_sem.at[4]),
-        pltpu.make_async_copy(contact_in, contacts.at[pl.ds(8, OWN)], in_sem.at[5]),
+        pltpu.make_async_copy(contact_in.at[face], marked, in_sem.at[5]),
         pltpu.make_async_copy(v_in, vs, in_sem.at[6]),
         pltpu.make_async_copy(forward_in, forward, in_sem.at[7]),
         pltpu.make_async_copy(inner_in, inner, in_sem.at[8]),
@@ -146,11 +147,23 @@
         pltpu.make_async_copy(inverse_in, inverse, in_sem.at[10]),
         pltpu.make_async_copy(unpack_in, unpack, in_sem.at[11]),
         pltpu.make_async_copy(twiddle_in, twiddle, in_sem.at[12]),
-        pltpu.make_async_copy(past_in, past, in_sem.at[13]),
-        pltpu.make_async_copy(newest_in, newest, in_sem.at[14]),
     ]
     for load in loads:
         load.start()
+    past_loads = []
+    for t in range(N2):
+        lanes = pl.ds(128 * t, 128)
+        past_loads += [
+            pltpu.make_async_copy(
+                history_in.at[face, pl.ds(0, 7), :, :, :, lanes], history.at[t], past_sem.at[0, t]
+            ),
+            pltpu.make_async_copy(kern_in.at[face, :, :, lanes], kern.at[t], past_sem.at[1, t]),
+        ]
+
+    @pl.when(plane)
+    def _():
+        for load in past_loads:
+            load.start()
 
     def strike_copies(i, src):
         return [
@@ -307,6 +320,7 @@
     marks = mm(flags[...].reshape(64, 32).astype(F32), widen[...]).reshape(8, 1, 8, 128)
     mods[1 : OWN + 1] = (stiff[...].reshape(8, 4, 8, 128) * (1.0 - 0.5 * marks)).reshape(OWN, 8, 128)
     loads[5].wait()
+    contacts[8 : OWN + 8] = marked[...].astype(F32)
 
     @pl.when(plane)
     def _():
@@ -320,6 +334,18 @@
     start_halo(0, us0)
     for copy in aux:
         copy.start()
+
+    @pl.when(plane)
+    def _():
+        for load in past_loads:
+            load.wait()
+        for c in range(3):
+            for q in range(2):
+                total = jnp.zeros((N2, 2, 128), F32)
+                for lag in range(7):
+                    weight = kern[:, c, lag + 1, :][:, None, :]
+                    total = total + weight * history[:, lag, q, c].astype(F32)
+                past[q, c] = total
 
     def substep(i, src, dst, offset):
         for c in range(3):
@@ -357,7 +383,12 @@
         tr, ti = twiddle[0], twiddle[1]
         turned = jnp.concatenate([re * tr - im * ti, re * ti + im * tr], axis=0)
         modes = mm(inner[...], turned)
-        modal_force = newest[...] * modes + past[...]
+        older = jnp.concatenate(
+            [past[q, c, :, dd, :] for q in range(2) for c in range(3) for dd in range(2)], axis=0
+        )
+        newest = jnp.concatenate([kern[:, c, 0, :] for c in range(3) for _ in range(2)], axis=0)
+        newest = jnp.concatenate([newest, newest], axis=0)
+        modal_force = newest * modes + older
         back = mm(outer[...], modal_force)
         re, im = back[:128], back[128:]
         turned = jnp.concatenate([re * tr + im * ti, im * tr - re * ti], axis=1)
@@ -420,24 +451,6 @@
             force[c, 4] = v1[8:40]
             force[c, 5] = v2[8:40]
 
-        @pl.when(low)
-        def _():
-            for k in range(3):
-                uf[:, :, k, :] = uf[:, :, k, :] + force[:, k]
-                vs[:, :, k, :] = vs[:, :, k, :] + force[:, 3 + k]
-
-        @pl.when(high)
-        def _():
-            for k in range(3):
-                uf[:, :, 7 - k, :] = uf[:, :, 7 - k, :] + force[:, k]
-                vs[:, :, 7 - k, :] = vs[:, :, 7 - k, :] + force[:, 3 + k]
-
-    stores = [
-        pltpu.make_async_copy(uf, u_out, out_sem.at[0]),
-        pltpu.make_async_copy(vs, v_out, out_sem.at[1]),
-    ]
-    for store in stores:
-        store.start()
     for i, src in enumerate((us0, us1, us2)):
         finish_halo(i, src)
     for copy in aux:
@@ -448,32 +461,61 @@
         for stage in stages:
             drain(stage)
 
-    for store in stores:
-        store.wait()
+
+def finish(uf, vs, force, u_out, v_out, u_new, v_new, sem):
+    m = lax.axis_index("normal")
+    low, high = m == 0, m == 7
+    plane = jnp.logical_or(low, high)
+
+    def store(a, b):
+        copies = [
+            pltpu.make_async_copy(a, u_out, sem.at[0]),
+            pltpu.make_async_copy(b, v_out, sem.at[1]),
+        ]
+        for copy in copies:
+            copy.start()
+        for copy in copies:
+            copy.wait()
+
+    @pl.when(jnp.logical_not(plane))
+    def _():
+        store(uf, vs)
+
+    @pl.when(plane)
+    def _():
+        u_new[...] = uf[...]
+        v_new[...] = vs[...]
+
+        @pl.when(low)
+        def _():
+            for k in range(3):
+                u_new[:, :, k, :] = uf[:, :, k, :] + force[:, k]
+                v_new[:, :, k, :] = vs[:, :, k, :] + force[:, 3 + k]
+
+        @pl.when(high)
+        def _():
+            for k in range(3):
+                u_new[:, :, 7 - k, :] = uf[:, :, 7 - k, :] + force[:, k]
+                v_new[:, :, 7 - k, :] = vs[:, :, 7 - k, :] + force[:, 3 + k]
+
+        store(u_new, v_new)
 
 
 def body(displacement, velocity, stiffness, yield_flags, contact, history, kern):
-    face = (lax.axis_index("normal") == lax.axis_size("normal") - 1).astype(jnp.int32)
-    own_history = lax.dynamic_index_in_dim(history, face, 0, keepdims=False)
-    own_kernel = lax.dynamic_index_in_dim(kern, face, 0, keepdims=False)
-    touching = lax.dynamic_index_in_dim(contact, face, 0, keepdims=False).astype(F32)
-    past = jnp.sum(own_kernel[1:, None, :, None, :] * own_history[:-1].astype(F32), axis=0)
-    past = past.reshape(192, 128)
-    newest = jnp.broadcast_to(own_kernel[0][None, :, None, :], (2, 3, 2, NS)).reshape(192, 128)
     any_space = pl.BlockSpec(memory_space=pl.ANY)
     dma, vmem = pltpu.SemaphoreType.DMA, pltpu.VMEM
     scratch = [
         vmem((3, OWN + 2, 8, 128), F32),
         vmem((3, OWN + 2, 8, 128), F32),
         vmem((3, OWN + 2, 8, 128), F32),
-        vmem((3, OWN, 8, 128), F32),
-        vmem((3, OWN, 8, 128), F32),
         vmem((OWN, 8, 128), F32),
         vmem((8, 8, 32), jnp.int32),
         vmem((OWN + 2, 8, 128), F32),
+        vmem((OWN, 128), jnp.int32),
         vmem((OWN + 16, 128), F32),
-        vmem((192, 128), F32),
-        vmem((192, 128), F32),
+        vmem((N2, 7, 2, 3, 2, 128), BF16),
+        vmem((N2, 3, 8, 128), F32),
+        vmem((2, 3, N2, 2, 128), F32),
         vmem((128, 256), BF16),
         vmem((192, 256), BF16),
         vmem((256, 192), BF16),
@@ -490,10 +532,9 @@
         vmem((NZ, GROUP, 4, 128), F32),
         vmem((NZ, GROUP, 4, 128), F32),
         vmem((GROUP, NZ, 4, 128), F32),
-        vmem((3, 6, OWN, 128), F32),
         vmem((3, OWN + 16, 128), F32),
-        dma((15,)),
-        dma((2,)),
+        dma((13,)),
+        dma((2, N2)),
         dma((4,)),
         dma((SUB, 4)),
         dma((SUB, 4)),
@@ -503,15 +544,27 @@
         dma((4, 8)),
     ]
     out = jax.ShapeDtypeStruct(displacement.shape, F32)
-    return pl.pallas_call(
+    in_vmem = pl.BlockSpec(memory_space=pltpu.VMEM)
+    pieces = pl.pallas_call(
         kernel,
-        out_shape=(out, out),
+        out_shape=(out, out, jax.ShapeDtypeStruct((3, 6, OWN, 128), F32)),
         in_specs=[any_space] * 15,
-        out_specs=(any_space, any_space),
+        out_specs=(in_vmem,) * 3,
         scratch_shapes=scratch,
         compiler_params=pltpu.CompilerParams(collective_id=0, has_side_effects=True),
         name="slab_step",
-    )(displacement, velocity, stiffness, yield_flags, touching, past, newest, *tables())
+    )(
+        displacement, velocity, stiffness, yield_flags, contact, history,
+        jnp.swapaxes(kern, 1, 2), *tables(),
+    )
+    return pl.pallas_call(
+        finish,
+        out_shape=(out, out),
+        in_specs=[in_vmem] * 3,
+        out_specs=(any_space, any_space),
+        scratch_shapes=[vmem(out.shape, F32), vmem(out.shape, F32), dma((2,))],
+        name="slab_finish",
+    )(*pieces)
 
 
 def solution(mesh):

time: 50.2 us -> 45.7 us (0.910)
  local copies, waits for them, and re-layouts: 4.21 us -> 0 us
  other arithmetic: 2.78 us -> 0 us
  Pallas kernels: 42.3 us -> 44.9 us
    unnamed x7 -> x0, local copies, waits for them, and re-layouts: 2.59 us -> none
    pallas_call x1 -> x2, Pallas kernels: 42.3 us -> 44.9 us  [the longest x1 42.5 us: body(): pl.pallas_call(kernel, out_shape=(out, out, jax.ShapeDtypeStruct((3, 6, O...]
    reshape x2 -> x0, local copies, waits for them, and re-layouts: 1.44 us -> none  [the longest x1 0.72 us: body(): jnp.broadcast_to(own_kernel[0][None, :, None, :], (2, 3, 2, NS))]
    reduce_sum x1 -> x0, other arithmetic: 1.42 us -> none  [body(): jnp.sum(own_kernel[1:, None, :, None, :] * own_history[:-1].astype(F32),...]
    convert_element_type x1 -> x0, other arithmetic: 1.37 us -> none  [body(): lax.dynamic_index_in_dim(contact, face, 0, keepdims=False).astype(F32)]
where the time goes in v1:
time: 45.7 us; the launch traced here: 45.6 us
  Pallas kernels  44.9 us (98%)
  between operations  0.64 us (1%)
    pallas_call x1, Pallas kernels, body(): pl.pallas_call(kernel, out_shape=(out, out, jax.ShapeDtypeStruct((3, 6, O...  42.5 us
    pallas_call x1, Pallas kernels, body(): pl.pallas_call(finish, out_shape=(out, out), in_specs=[in_vmem] * 3, out_...  2.45 us

profile of v1, /device:TPU:2, one launch (start us, length us, event | category | flops | bytes accessed | tf_op | source)
XLA Modules:
  0.0 45.6 jit_solution(9012986952602034881)
XLA Ops:
  0.6 42.5 %slab_step.1 = (f32[3,32,8,128]{3,2,1,0:T(8,128)}, f32[3,32,8,128]{3,2,1,0:T(8,128)}, f32[3,6,32,128]{3,2,1,0:T(8,128)}) custom-call(f32[3,32,8,128]{3,2,1,0:T(8,128)} %u_in.1, f32[3,32,8,128]{3,2,1,0:T(8,128)} %v_in.1, f32[32,8,128]{2,1,0:T(8,128)} %stiff_in.1, s32[8,8,32]{2,1,0:T(8,128)} %flags_in.1, s32[2,32,128]{2,1,0:T(8,128)} %contact_in.1, ...), custom_call_target="tpu_custom_call" | custom-call | tf_op jit(solution)/shard_map/slab_step/pallas_call | solution.py:548
  43.1 2.5 %slab_finish.1 = (f32[3,32,8,128]{3,2,1,0:T(8,128)}, f32[3,32,8,128]{3,2,1,0:T(8,128)}) custom-call(f32[3,32,8,128]{3,2,1,0:T(8,128)} %get-tuple-element.5.uf, f32[3,32,8,128]{3,2,1,0:T(8,128)} %get-tuple-element.6.vs, f32[3,6,32,128]{3,2,1,0:T(8,128)} %get-tuple-element.7.force), custom_call_target="tpu_custom_call" | custom-call | tf_op jit(solution)/shard_map/slab_finish/pallas_call | solution.py:560

commit v2 on v1

--- a/solution.py
+++ b/solution.py
@@ -19,6 +19,7 @@
 OWN = 32
 NS = SLABS * OWN
 N1, N2 = 128, 16
+GRANT = 16 * 2**20
 F32, BF16 = jnp.float32, jnp.bfloat16
 
 
@@ -33,9 +34,9 @@
     first = np.concatenate([2 * slab_bz, 2 * slab_bz + 1])
     angle = 2 * np.pi * (np.outer(first, k1) % N1) / N1
     forward = np.concatenate([np.cos(angle), -np.sin(angle)], axis=1)
-    twist = 2 * np.pi * np.outer(n2, k1) / NS / 1.0
+    twist = 2 * np.pi * np.outer(n2, k1) / NS
     norm = 1.0 / math.sqrt(NS)
-    twiddle = norm * np.stack([np.tile(np.cos(twist), (8, 1)), np.tile(-np.sin(twist), (8, 1))])
+    turn = [np.tile(np.cos(twist), (8, 1)), np.tile(-np.sin(twist), (8, 1))]
     small = 2 * np.pi * (np.outer(t, n2) % N2) / N2
     co, si = np.cos(small), np.sin(small)
     inner = np.zeros((2, 3, 2, N2, 2, 2, 4, N2))
@@ -50,9 +51,21 @@
             outer[0, dd, c, :, 1, c, dd, :] = -si.T
             outer[1, dd, c, :, 0, c, dd, :] = si.T
             outer[1, dd, c, :, 1, c, dd, :] = co.T
+    node = np.concatenate([np.tile(n2, 3), np.zeros(N2, np.int64)])
+    for i in range(12):
+        c, beyond = (i % 6) // 2, (i % 2) + (16 if i >= 6 else -2)
+        node[3 * N2 + i] = beyond
+        edge = 2 * np.pi * ((t * beyond) % N2) / N2
+        for dd in range(2):
+            outer[0, dd, 3, i, 0, c, dd, :] = np.cos(edge)
+            outer[0, dd, 3, i, 1, c, dd, :] = -np.sin(edge)
+            outer[1, dd, 3, i, 0, c, dd, :] = np.sin(edge)
+            outer[1, dd, 3, i, 1, c, dd, :] = np.cos(edge)
+    untwist = 2 * np.pi * np.outer(np.tile(node, 2), k1) / NS
+    twiddle = norm * np.stack(turn + [np.cos(untwist), np.sin(untwist)])
     inner = inner.reshape(192, 256)
     outer = outer.reshape(256, 192)
-    last = np.concatenate([2 * slab_zb - 1 + r for r in range(4)]) % N1
+    last = np.concatenate([2 * slab_zb, 2 * slab_zb + 1])
     angle = 2 * np.pi * (np.outer(last, k1) % N1) / N1
     inverse = np.concatenate([np.cos(angle), -np.sin(angle)], axis=1)
     dips = np.arange(128)[None, :]
@@ -89,7 +102,7 @@
     uf, vs, force,
     us0, us1, us2, stiff, flags, mods, marked, contacts, history, kern, past,
     forward, inner, outer, inverse, pack, unpack, widen, twiddle,
-    faces, sides, p1, g1, r1, p2, g2, q2, mod2,
+    faces, sides, p1, g1, r1, p2, g2, q2, wide, pulls, mod2,
     in_sem, past_sem, self_sem, halo_s, halo_r, aux_s, aux_r, a2a_s, a2a_r,
 ):
     s = lax.axis_index("strike")
@@ -302,7 +315,8 @@
             rows.append(jnp.zeros((16, 128), F32))
             block = jnp.concatenate(rows, axis=0)
             halves = [mm_nt(pack[dd], block) for dd in range(2)]
-            p1[:, :, jh, :] = jnp.concatenate(halves, axis=1).reshape(NZ, GROUP, 128)
+            wide[:, :, jh, :] = jnp.concatenate(halves, axis=1).reshape(NZ, GROUP, 128)
+        p1[...] = wide[...].astype(BF16)
 
     @pl.when(low)
     def _():
@@ -377,7 +391,8 @@
     @pl.when(plane)
     def _():
         land(stages[1])
-        got = jnp.concatenate([r1[:, :, jh, :].reshape(SLABS, 128) for jh in range(2)], axis=0)
+        wide[...] = r1[...].astype(F32)
+        got = jnp.concatenate([wide[:, :, jh, :].reshape(SLABS, 128) for jh in range(2)], axis=0)
         y = mm(got.T, forward[...])
         re, im = y[:, :128], y[:, 128:]
         tr, ti = twiddle[0], twiddle[1]
@@ -391,10 +406,12 @@
         modal_force = newest * modes + older
         back = mm(outer[...], modal_force)
         re, im = back[:128], back[128:]
-        turned = jnp.concatenate([re * tr + im * ti, im * tr - re * ti], axis=1)
+        tr, ti = twiddle[2], twiddle[3]
+        turned = jnp.concatenate([re * tr - im * ti, re * ti + im * tr], axis=1)
         pulled = mm_nt(inverse[...], turned)
-        for r in range(4):
-            p2[:, :, r, :] = pulled[64 * r : 64 * r + 64].reshape(NZ, GROUP, 128)
+        for jh in range(2):
+            wide[:, :, jh, :] = pulled[64 * jh : 64 * jh + 64].reshape(NZ, GROUP, 128)
+        p2[...] = wide[...].astype(BF16)
         launch(stages[2])
 
     wait_halo(1, us1)
@@ -415,12 +432,14 @@
     @pl.when(plane)
     def _():
         mod2[...] = jnp.zeros_like(mod2)
+        pulls[...] = jnp.zeros_like(pulls)
         for k in range(3):
             mod2[k, 7:41] = jnp.where(high, mods[:, 7 - k, :], mods[:, k, :])
         land(stages[3])
+        wide[...] = q2[...].astype(F32)
         pieces = []
-        for r in range(4):
-            turned = q2[:, :, r, :].reshape(SLABS, 128).T
+        for jh in range(2):
+            turned = wide[:, :, jh, :].reshape(SLABS, 128).T
             pieces.append(mm(turned[:64], unpack[0]) + mm(turned[64:], unpack[1]))
 
         def lap2(x):
@@ -429,11 +448,11 @@
         half = time_step
         for c in range(3):
             a = 16 * c
-            load = contacts[...] * jnp.concatenate(
-                [pieces[0][a + 8 : a + 16], pieces[1][a : a + 16],
-                 pieces[2][a : a + 16], pieces[3][a : a + 8]],
-                axis=0,
-            )
+            pulls[c, 6:8] = pieces[0][48 + 2 * c : 50 + 2 * c]
+            pulls[c, 8:24] = pieces[0][a : a + 16]
+            pulls[c, 24:40] = pieces[1][a : a + 16]
+            pulls[c, 40:42] = pieces[1][54 + 2 * c : 56 + 2 * c]
+            load = contacts[...] * pulls[c]
             v0 = half * load
             u0 = half * v0
             v0, v1 = v0 + half * (mod2[0] * lap2(u0) + load), half * (mod2[1] * u0)
@@ -519,19 +538,21 @@
         vmem((128, 256), BF16),
         vmem((192, 256), BF16),
         vmem((256, 192), BF16),
-        vmem((256, 256), BF16),
+        vmem((128, 256), BF16),
         vmem((2, 64, 128), BF16),
         vmem((2, 64, 128), BF16),
         vmem((32, 128), BF16),
-        vmem((2, 128, 128), F32),
+        vmem((4, 128, 128), F32),
         vmem((SUB, 2, 3, OWN, 128), F32),
         vmem((SUB, 2, 3, OWN, 128), F32),
+        vmem((NZ, GROUP, 2, 128), BF16),
+        vmem((NZ, GROUP, 2, 128), BF16),
+        vmem((GROUP, NZ, 2, 128), BF16),
+        vmem((NZ, GROUP, 2, 128), BF16),
+        vmem((NZ, GROUP, 2, 128), BF16),
+        vmem((GROUP, NZ, 2, 128), BF16),
         vmem((NZ, GROUP, 2, 128), F32),
-        vmem((NZ, GROUP, 2, 128), F32),
-        vmem((GROUP, NZ, 2, 128), F32),
-        vmem((NZ, GROUP, 4, 128), F32),
-        vmem((NZ, GROUP, 4, 128), F32),
-        vmem((GROUP, NZ, 4, 128), F32),
+        vmem((3, OWN + 16, 128), F32),
         vmem((3, OWN + 16, 128), F32),
         dma((13,)),
         dma((2, N2)),
@@ -545,17 +566,20 @@
     ]
     out = jax.ShapeDtypeStruct(displacement.shape, F32)
     in_vmem = pl.BlockSpec(memory_space=pltpu.VMEM)
+    fix = lambda x: pltpu.with_memory_space_constraint(x, pltpu.HBM)
     pieces = pl.pallas_call(
         kernel,
         out_shape=(out, out, jax.ShapeDtypeStruct((3, 6, OWN, 128), F32)),
         in_specs=[any_space] * 15,
         out_specs=(in_vmem,) * 3,
         scratch_shapes=scratch,
-        compiler_params=pltpu.CompilerParams(collective_id=0, has_side_effects=True),
+        compiler_params=pltpu.CompilerParams(
+            collective_id=0, has_side_effects=True, vmem_limit_bytes=GRANT
+        ),
         name="slab_step",
     )(
-        displacement, velocity, stiffness, yield_flags, contact, history,
-        jnp.swapaxes(kern, 1, 2), *tables(),
+        *map(fix, (displacement, velocity, stiffness, yield_flags, contact, history)),
+        fix(jnp.swapaxes(kern, 1, 2)), *map(fix, tables()),
     )
     return pl.pallas_call(
         finish,
@@ -563,6 +587,7 @@
         in_specs=[in_vmem] * 3,
         out_specs=(any_space, any_space),
         scratch_shapes=[vmem(out.shape, F32), vmem(out.shape, F32), dma((2,))],
+        compiler_params=pltpu.CompilerParams(vmem_limit_bytes=GRANT),
         name="slab_finish",
     )(*pieces)
 

time: 45.7 us -> 42.1 us (0.921)
  Pallas kernels: 44.9 us -> 41.3 us
    pallas_call x1, Pallas kernels: 42.5 us -> 40 us  [body(): pl.pallas_call(kernel, out_shape=(out, out, jax.ShapeDtypeStruct((3, 6, O...]
    pallas_call x1, Pallas kernels: 2.45 us -> 1.26 us  [body(): pl.pallas_call(finish, out_shape=(out, out), in_specs=[in_vmem] * 3, out_...]
where the time goes in v2:
time: 42.1 us; the launch traced here: 41.9 us
  Pallas kernels  41.3 us (98%)
  between operations  0.64 us (2%)
    pallas_call x1, Pallas kernels, body(): pl.pallas_call(kernel, out_shape=(out, out, jax.ShapeDtypeStruct((3, 6, O...  40 us
    pallas_call x1, Pallas kernels, body(): pl.pallas_call(finish, out_shape=(out, out), in_specs=[in_vmem] * 3, out_...  1.26 us

profile of v2, /device:TPU:2, one launch (start us, length us, event | category | flops | bytes accessed | tf_op | source)
XLA Modules:
  0.0 41.9 jit_solution(7068049651753841432)
XLA Ops:
  0.6 40.0 %slab_step.1 = (f32[3,32,8,128]{3,2,1,0:T(8,128)S(1)}, f32[3,32,8,128]{3,2,1,0:T(8,128)S(1)}, f32[3,6,32,128]{3,2,1,0:T(8,128)S(1)}) custom-call(f32[3,32,8,128]{3,2,1,0:T(8,128)} %u_in.1, f32[3,32,8,128]{3,2,1,0:T(8,128)} %v_in.1, f32[32,8,128]{2,1,0:T(8,128)} %stiff_in.1, s32[8,8,32]{2,1,0:T(8,128)} %flags_in.1, s32[2,32,128]{2,1,0:T(8,128)} %contact_in.1, ...), custom_call_target="tpu_custom_call" | custom-call | tf_op jit(solution)/shard_map/slab_step/pallas_call | solution.py:570
  40.7 1.3 %slab_finish.1 = (f32[3,32,8,128]{3,2,1,0:T(8,128)}, f32[3,32,8,128]{3,2,1,0:T(8,128)}) custom-call(f32[3,32,8,128]{3,2,1,0:T(8,128)S(1)} %get-tuple-element.5.uf, f32[3,32,8,128]{3,2,1,0:T(8,128)S(1)} %get-tuple-element.6.vs, f32[3,6,32,128]{3,2,1,0:T(8,128)S(1)} %get-tuple-element.7.force), custom_call_target="tpu_custom_call" | custom-call | tf_op jit(solution)/shard_map/slab_finish/pallas_call | solution.py:584

commit v3 on v2

--- a/solution.py
+++ b/solution.py
@@ -27,11 +27,13 @@
     z = np.arange(NZ)[:, None]
     b = np.arange(GROUP)[None, :]
     slab_zb = ((b // NX) * (NZ * NX) + z * NX + b % NX).reshape(-1)
-    slab_bz = ((b // NX) * (NZ * NX) + z * NX + b % NX).T.reshape(-1)
+    x4, h2, z8 = np.arange(NX), np.arange(YH), np.arange(NZ)
+    slab_xhz = (h2[None, :, None] * (NZ * NX) + z8 * NX + x4[:, None, None]).reshape(-1)
+    slab_xzh = (h2 * (NZ * NX) + z8[None, :, None] * NX + x4[:, None, None]).reshape(-1)
     k1 = np.arange(N1)
     n2 = np.arange(N2)
     t = np.arange(N2)
-    first = np.concatenate([2 * slab_bz, 2 * slab_bz + 1])
+    first = np.concatenate([2 * slab_zb, 2 * slab_zb + 1])
     angle = 2 * np.pi * (np.outer(first, k1) % N1) / N1
     forward = np.concatenate([np.cos(angle), -np.sin(angle)], axis=1)
     twist = 2 * np.pi * np.outer(n2, k1) / NS
@@ -69,8 +71,8 @@
     angle = 2 * np.pi * (np.outer(last, k1) % N1) / N1
     inverse = np.concatenate([np.cos(angle), -np.sin(angle)], axis=1)
     dips = np.arange(128)[None, :]
-    pack = np.stack([dips == 2 * slab_zb[:, None] + dd for dd in range(2)])
-    unpack = np.stack([dips == 2 * slab_bz[:, None] + dd for dd in range(2)])
+    pack = np.stack([dips == 2 * slab_xhz[:, None] + dd for dd in range(2)])
+    unpack = np.stack([dips == 2 * slab_xzh[:, None] + dd for dd in range(2)])
     widen = np.arange(32)[:, None] == dips // 4
     bf = [forward, inner, outer, inverse, pack, unpack, widen]
     return [jnp.asarray(a.astype(np.float32), dtype=BF16) for a in bf] + [
@@ -114,6 +116,14 @@
     face = m // 7
     left, right = (s + SLABS - 1) % SLABS, (s + 1) % SLABS
     mine_b_base = (my_b // NX) * (NZ * NX) + my_b % NX
+    my_x = s % NX
+    early = my_b < NX
+    owner = jnp.logical_and(plane, early)
+    feeder = jnp.logical_and(plane, jnp.logical_not(early))
+
+    def x_peer(i):
+        x = (my_x + i) % NX
+        return x, my_z * NX + x
 
     def z_peer(i):
         z = (my_z + i) % NZ
@@ -139,12 +149,17 @@
     def _():
         greet(normal=m + 1)
 
-    @pl.when(plane)
+    @pl.when(owner)
     def _():
         for i in range(1, NZ):
             greet(strike=z_peer(i)[1])
         for i in range(1, GROUP):
             greet(strike=b_peer(i)[1])
+
+    @pl.when(feeder)
+    def _():
+        for i in range(NX):
+            greet(strike=x_peer(i)[1])
 
     loads = [
         pltpu.make_async_copy(u_in, us0.at[:, pl.ds(1, OWN)], in_sem.at[0]),
@@ -261,45 +276,76 @@
         ),
     ]
 
-    def z_copies(k, src, dst):
-        copies = []
-        for i in range(1, NZ):
-            z, who = z_peer(i)
-            copies.append(
-                pltpu.make_async_remote_copy(
-                    src.at[z], dst.at[my_z], a2a_s.at[k, i], a2a_r.at[k, i],
-                    device_id={"strike": who}, device_id_type=MESH,
-                )
-            )
-        return copies, pltpu.make_async_copy(src.at[my_z], dst.at[my_z], self_sem.at[k])
-
-    def b_copies(k, src, dst):
-        copies = []
-        for i in range(1, GROUP):
-            b, who = b_peer(i)
-            copies.append(
-                pltpu.make_async_remote_copy(
-                    src.at[:, b], dst.at[my_b], a2a_s.at[k, i], a2a_r.at[k, i],
-                    device_id={"strike": who}, device_id_type=MESH,
-                )
-            )
-        return copies, pltpu.make_async_copy(src.at[:, my_b], dst.at[my_b], self_sem.at[k])
-
-    def launch(stage):
-        for copy in stage[0]:
+    def send(k, i, j, src, dst, who):
+        return pltpu.make_async_remote_copy(
+            src, dst, a2a_s.at[k, i], a2a_r.at[k, j],
+            device_id={"strike": who}, device_id_type=MESH,
+        )
+
+    def gather_sends(first):
+        return [
+            send(0, i, my_b, p1.at[x_peer(i)[0]], g1.at[my_b], x_peer(i)[1])
+            for i in range(first, NX)
+        ]
+
+    def gather_self():
+        return pltpu.make_async_copy(p1.at[my_x], g1.at[my_b], self_sem.at[0])
+
+    def gather_lands():
+        return [
+            send(0, 0, b_peer(i)[0], p1.at[0], g1.at[b_peer(i)[0]], s ^ 1)
+            for i in range(1, GROUP)
+        ]
+
+    def turn_sends():
+        return [
+            send(1, i, i, g1.at[:, :, z_peer(i)[0]], r1.at[my_z], z_peer(i)[1])
+            for i in range(1, NZ)
+        ]
+
+    def turn_self():
+        return pltpu.make_async_copy(g1.at[:, :, my_z], r1.at[my_z], self_sem.at[1])
+
+    def return_sends():
+        return [
+            send(2, i, i, p2.at[z_peer(i)[0]], g2.at[my_z], z_peer(i)[1]) for i in range(1, NZ)
+        ]
+
+    def return_self():
+        return pltpu.make_async_copy(p2.at[my_z], g2.at[my_z], self_sem.at[2])
+
+    def scatter_sends():
+        return [
+            send(3, i, my_x, g2.at[:, b_peer(i)[0]], q2.at[my_x], b_peer(i)[1])
+            for i in range(1, GROUP)
+        ]
+
+    def scatter_self():
+        return pltpu.make_async_copy(g2.at[:, my_b], q2.at[my_x], self_sem.at[3])
+
+    def scatter_lands(first):
+        return [
+            send(3, 0, x_peer(i)[0], g2.at[:, 0], q2.at[x_peer(i)[0]], s ^ 1)
+            for i in range(first, NX)
+        ]
+
+    def past_copy(who):
+        return pltpu.make_async_remote_copy(
+            past.at[0], past.at[1], aux_s.at[4], aux_r.at[4],
+            device_id={"strike": who}, device_id_type=MESH,
+        )
+
+    def start_all(copies):
+        for copy in copies:
             copy.start()
-        stage[1].start()
-
-    def land(stage):
-        for copy in stage[0]:
+
+    def recv_all(copies):
+        for copy in copies:
             copy.wait_recv()
-        stage[1].wait()
-
-    def drain(stage):
-        for copy in stage[0]:
+
+    def sent_all(copies):
+        for copy in copies:
             copy.wait_send()
-
-    stages = [z_copies(0, p1, g1), b_copies(1, g1, r1), z_copies(2, p2, g2), b_copies(3, g2, q2)]
 
     loads[0].wait()
     set_faces(0, us0)
@@ -316,7 +362,7 @@
             block = jnp.concatenate(rows, axis=0)
             halves = [mm_nt(pack[dd], block) for dd in range(2)]
             wide[:, :, jh, :] = jnp.concatenate(halves, axis=1).reshape(NZ, GROUP, 128)
-        p1[...] = wide[...].astype(BF16)
+        p1[...] = wide[...].reshape(NX, YH, NZ, 2, 128).astype(BF16)
 
     @pl.when(low)
     def _():
@@ -336,10 +382,16 @@
     loads[5].wait()
     contacts[8 : OWN + 8] = marked[...].astype(F32)
 
-    @pl.when(plane)
+    @pl.when(owner)
     def _():
         pl.semaphore_wait(barrier, 3 + NZ - 1 + GROUP - 1)
-        launch(stages[0])
+        start_all(gather_sends(1))
+        gather_self().start()
+
+    @pl.when(feeder)
+    def _():
+        pl.semaphore_wait(barrier, 3 + NX)
+        start_all(gather_sends(0))
 
     @pl.when(jnp.logical_not(plane))
     def _():
@@ -359,7 +411,11 @@
                 for lag in range(7):
                     weight = kern[:, c, lag + 1, :][:, None, :]
                     total = total + weight * history[:, lag, q, c].astype(F32)
-                past[q, c] = total
+                past[0, q, c] = total
+
+    @pl.when(feeder)
+    def _():
+        past_copy(s - NZ * NX).start()
 
     def substep(i, src, dst, offset):
         for c in range(3):
@@ -374,10 +430,12 @@
             vs[c] = speed
             dst[c, offset : offset + OWN] = here + time_step * speed
 
-    @pl.when(plane)
-    def _():
-        land(stages[0])
-        launch(stages[1])
+    @pl.when(owner)
+    def _():
+        recv_all(gather_lands())
+        gather_self().wait()
+        start_all(turn_sends())
+        turn_self().start()
 
     loads[6].wait()
     wait_halo(0, us0)
@@ -388,42 +446,47 @@
     for load in loads[7:]:
         load.wait()
 
-    @pl.when(plane)
-    def _():
-        land(stages[1])
-        wide[...] = r1[...].astype(F32)
-        got = jnp.concatenate([wide[:, :, jh, :].reshape(SLABS, 128) for jh in range(2)], axis=0)
-        y = mm(got.T, forward[...])
-        re, im = y[:, :128], y[:, 128:]
-        tr, ti = twiddle[0], twiddle[1]
-        turned = jnp.concatenate([re * tr - im * ti, re * ti + im * tr], axis=0)
-        modes = mm(inner[...], turned)
-        older = jnp.concatenate(
-            [past[q, c, :, dd, :] for q in range(2) for c in range(3) for dd in range(2)], axis=0
-        )
+    @pl.when(owner)
+    def _():
         newest = jnp.concatenate([kern[:, c, 0, :] for c in range(3) for _ in range(2)], axis=0)
         newest = jnp.concatenate([newest, newest], axis=0)
-        modal_force = newest * modes + older
-        back = mm(outer[...], modal_force)
-        re, im = back[:128], back[128:]
-        tr, ti = twiddle[2], twiddle[3]
-        turned = jnp.concatenate([re * tr - im * ti, re * ti + im * tr], axis=1)
-        pulled = mm_nt(inverse[...], turned)
-        for jh in range(2):
-            wide[:, :, jh, :] = pulled[64 * jh : 64 * jh + 64].reshape(NZ, GROUP, 128)
-        p2[...] = wide[...].astype(BF16)
-        launch(stages[2])
+        recv_all(turn_sends())
+        turn_self().wait()
+        past_copy(s ^ 1).wait_recv()
+        for h in range(YH):
+            wide[...] = r1[:, :, h].astype(F32)
+            got = jnp.concatenate(
+                [wide[:, :, jh, :].reshape(SLABS, 128) for jh in range(2)], axis=0
+            )
+            y = mm(got.T, forward[...])
+            re, im = y[:, :128], y[:, 128:]
+            tr, ti = twiddle[0], twiddle[1]
+            turned = jnp.concatenate([re * tr - im * ti, re * ti + im * tr], axis=0)
+            modes = mm(inner[...], turned)
+            older = jnp.concatenate(
+                [past[h, q, c, :, dd, :] for q in range(2) for c in range(3) for dd in range(2)],
+                axis=0,
+            )
+            back = mm(outer[...], newest * modes + older)
+            re, im = back[:128], back[128:]
+            tr, ti = twiddle[2], twiddle[3]
+            turned = jnp.concatenate([re * tr - im * ti, re * ti + im * tr], axis=1)
+            pulled = mm_nt(inverse[...], turned)
+            for jh in range(2):
+                wide[:, :, jh, :] = pulled[64 * jh : 64 * jh + 64].reshape(NZ, GROUP, 128)
+            p2[:, :, h] = wide[...].astype(BF16)
+        start_all(return_sends())
+        return_self().start()
+        recv_all(return_sends())
+        return_self().wait()
+        start_all(scatter_sends())
+        scatter_self().start()
 
     wait_halo(1, us1)
     substep(1, us1, us2, 1)
     set_faces(2, us2)
     start_halo(2, us2)
 
-    @pl.when(plane)
-    def _():
-        land(stages[2])
-        launch(stages[3])
-
     wait_halo(2, us2)
     substep(2, us2, uf, 0)
     for copy in aux:
@@ -435,8 +498,19 @@
         pulls[...] = jnp.zeros_like(pulls)
         for k in range(3):
             mod2[k, 7:41] = jnp.where(high, mods[:, 7 - k, :], mods[:, k, :])
-        land(stages[3])
-        wide[...] = q2[...].astype(F32)
+
+    @pl.when(owner)
+    def _():
+        recv_all(scatter_lands(1))
+        scatter_self().wait()
+
+    @pl.when(feeder)
+    def _():
+        recv_all(scatter_lands(0))
+
+    @pl.when(plane)
+    def _():
+        wide[...] = q2[...].astype(F32).reshape(NZ, GROUP, 2, 128)
         pieces = []
         for jh in range(2):
             turned = wide[:, :, jh, :].reshape(SLABS, 128).T
@@ -475,10 +549,14 @@
     for copy in aux:
         copy.wait_send()
 
-    @pl.when(plane)
-    def _():
-        for stage in stages:
-            drain(stage)
+    @pl.when(owner)
+    def _():
+        sent_all(gather_sends(1) + turn_sends() + return_sends() + scatter_sends())
+
+    @pl.when(feeder)
+    def _():
+        sent_all(gather_sends(0))
+        past_copy(s - NZ * NX).wait_send()
 
 
 def finish(uf, vs, force, u_out, v_out, u_new, v_new, sem):
@@ -534,7 +612,7 @@
         vmem((OWN + 16, 128), F32),
         vmem((N2, 7, 2, 3, 2, 128), BF16),
         vmem((N2, 3, 8, 128), F32),
-        vmem((2, 3, N2, 2, 128), F32),
+        vmem((2, 2, 3, N2, 2, 128), F32),
         vmem((128, 256), BF16),
         vmem((192, 256), BF16),
         vmem((256, 192), BF16),
@@ -545,12 +623,12 @@
         vmem((4, 128, 128), F32),
         vmem((SUB, 2, 3, OWN, 128), F32),
         vmem((SUB, 2, 3, OWN, 128), F32),
-        vmem((NZ, GROUP, 2, 128), BF16),
-        vmem((NZ, GROUP, 2, 128), BF16),
-        vmem((GROUP, NZ, 2, 128), BF16),
-        vmem((NZ, GROUP, 2, 128), BF16),
-        vmem((NZ, GROUP, 2, 128), BF16),
-        vmem((GROUP, NZ, 2, 128), BF16),
+        vmem((NX, YH, NZ, 2, 128), BF16),
+        vmem((GROUP, YH, NZ, 2, 128), BF16),
+        vmem((NZ, GROUP, YH, 2, 128), BF16),
+        vmem((NZ, GROUP, YH, 2, 128), BF16),
+        vmem((NZ, GROUP, YH, 2, 128), BF16),
+        vmem((NX, NZ, YH, 2, 128), BF16),
         vmem((NZ, GROUP, 2, 128), F32),
         vmem((3, OWN + 16, 128), F32),
         vmem((3, OWN + 16, 128), F32),
@@ -559,8 +637,8 @@
         dma((4,)),
         dma((SUB, 4)),
         dma((SUB, 4)),
-        dma((4,)),
-        dma((4,)),
+        dma((5,)),
+        dma((5,)),
         dma((4, 8)),
         dma((4, 8)),
     ]

time: 42.1 us -> 39.3 us (0.933)
  the two profiles are of different devices: /device:TPU:2 before, /device:TPU:32 now
where the time goes in v3:
time: 39.3 us; the launch traced here: 39.2 us
  Pallas kernels  38.6 us (98%)
  between operations  0.64 us (2%)
    pallas_call x1, Pallas kernels, body(): pl.pallas_call(kernel, out_shape=(out, out, jax.ShapeDtypeStruct((3, 6, O...  37.3 us
    pallas_call x1, Pallas kernels, body(): pl.pallas_call(finish, out_shape=(out, out), in_specs=[in_vmem] * 3, out_...  1.26 us

profile of v3, /device:TPU:32, one launch (start us, length us, event | category | flops | bytes accessed | tf_op | source)
XLA Modules:
  0.0 39.2 jit_solution(10827717107776730315)
XLA Ops:
  0.6 37.3 %slab_step.1 = (f32[3,32,8,128]{3,2,1,0:T(8,128)S(1)}, f32[3,32,8,128]{3,2,1,0:T(8,128)S(1)}, f32[3,6,32,128]{3,2,1,0:T(8,128)S(1)}) custom-call(f32[3,32,8,128]{3,2,1,0:T(8,128)} %u_in.1, f32[3,32,8,128]{3,2,1,0:T(8,128)} %v_in.1, f32[32,8,128]{2,1,0:T(8,128)} %stiff_in.1, s32[8,8,32]{2,1,0:T(8,128)} %flags_in.1, s32[2,32,128]{2,1,0:T(8,128)} %contact_in.1, ...), custom_call_target="tpu_custom_call" | custom-call | tf_op jit(solution)/shard_map/slab_step/pallas_call | solution.py:648
  37.9 1.3 %slab_finish.1 = (f32[3,32,8,128]{3,2,1,0:T(8,128)}, f32[3,32,8,128]{3,2,1,0:T(8,128)}) custom-call(f32[3,32,8,128]{3,2,1,0:T(8,128)S(1)} %get-tuple-element.5.uf, f32[3,32,8,128]{3,2,1,0:T(8,128)S(1)} %get-tuple-element.6.vs, f32[3,6,32,128]{3,2,1,0:T(8,128)S(1)} %get-tuple-element.7.force), custom_call_target="tpu_custom_call" | custom-call | tf_op jit(solution)/shard_map/slab_finish/pallas_call | solution.py:662

commit v4 on v3

--- a/solution.py
+++ b/solution.py
@@ -17,6 +17,7 @@
 GROUP = YH * NX
 SLABS = YH * NZ * NX
 OWN = 32
+WIDE = OWN + 4
 NS = SLABS * OWN
 N1, N2 = 128, 16
 GRANT = 16 * 2**20
@@ -101,10 +102,10 @@
 def kernel(
     u_in, v_in, stiff_in, flags_in, contact_in, history_in, kern_in,
     forward_in, inner_in, outer_in, inverse_in, pack_in, unpack_in, widen_in, twiddle_in,
-    uf, vs, force,
-    us0, us1, us2, stiff, flags, mods, marked, contacts, history, kern, past,
+    uf, vs,
+    us0, us1, us2, vx, vy, stiff, flags, mods, marked, contacts, history, kern, past,
     forward, inner, outer, inverse, pack, unpack, widen, twiddle,
-    faces, sides, p1, g1, r1, p2, g2, q2, wide, pulls, mod2,
+    faces, sides, p1, g1, r1, p2, g2, q2, wide, spread, pulls, mod2,
     in_sem, past_sem, self_sem, halo_s, halo_r, aux_s, aux_r, a2a_s, a2a_r,
 ):
     s = lax.axis_index("strike")
@@ -162,13 +163,13 @@
             greet(strike=x_peer(i)[1])
 
     loads = [
-        pltpu.make_async_copy(u_in, us0.at[:, pl.ds(1, OWN)], in_sem.at[0]),
+        pltpu.make_async_copy(u_in, us0.at[:, pl.ds(3, OWN)], in_sem.at[0]),
         pltpu.make_async_copy(pack_in, pack, in_sem.at[1]),
         pltpu.make_async_copy(flags_in, flags, in_sem.at[2]),
         pltpu.make_async_copy(stiff_in, stiff, in_sem.at[3]),
         pltpu.make_async_copy(widen_in, widen, in_sem.at[4]),
         pltpu.make_async_copy(contact_in.at[face], marked, in_sem.at[5]),
-        pltpu.make_async_copy(v_in, vs, in_sem.at[6]),
+        pltpu.make_async_copy(v_in, vx.at[:, pl.ds(2, OWN)], in_sem.at[6]),
         pltpu.make_async_copy(forward_in, forward, in_sem.at[7]),
         pltpu.make_async_copy(inner_in, inner, in_sem.at[8]),
         pltpu.make_async_copy(outer_in, outer, in_sem.at[9]),
@@ -188,39 +189,38 @@
             pltpu.make_async_copy(kern_in.at[face, :, :, lanes], kern.at[t], past_sem.at[1, t]),
         ]
 
-    @pl.when(plane)
-    def _():
-        for load in past_loads:
-            load.start()
-
-    def strike_copies(i, src):
-        return [
-            pltpu.make_async_remote_copy(
-                src.at[:, OWN], src.at[:, 0], halo_s.at[i, 0], halo_r.at[i, 0],
-                device_id={"strike": right}, device_id_type=MESH,
-            ),
-            pltpu.make_async_remote_copy(
-                src.at[:, 1], src.at[:, OWN + 1], halo_s.at[i, 1], halo_r.at[i, 1],
-                device_id={"strike": left}, device_id_type=MESH,
-            ),
-        ]
+    def strike_copies():
+        copies = []
+        for k, (ref, depth) in enumerate(((us0, 3), (vx, 2), (mods, 2))):
+            def part(start, ref=ref, depth=depth):
+                window = pl.ds(start, depth)
+                return ref.at[window] if ref is mods else ref.at[:, window]
+
+            copies += [
+                pltpu.make_async_remote_copy(
+                    part(OWN), part(0), aux_s.at[2 * k], aux_r.at[2 * k],
+                    device_id={"strike": right}, device_id_type=MESH,
+                ),
+                pltpu.make_async_remote_copy(
+                    part(depth), part(OWN + depth), aux_s.at[2 * k + 1], aux_r.at[2 * k + 1],
+                    device_id={"strike": left}, device_id_type=MESH,
+                ),
+            ]
+        return copies
 
     def up_copy(i):
         return pltpu.make_async_remote_copy(
-            faces.at[i, 1], sides.at[i, 0], halo_s.at[i, 2], halo_r.at[i, 2],
+            faces.at[i, 1], sides.at[i, 0], halo_s.at[i, 0], halo_r.at[i, 0],
             device_id={"normal": m + 1}, device_id_type=MESH,
         )
 
     def down_copy(i):
         return pltpu.make_async_remote_copy(
-            faces.at[i, 0], sides.at[i, 1], halo_s.at[i, 3], halo_r.at[i, 3],
+            faces.at[i, 0], sides.at[i, 1], halo_s.at[i, 1], halo_r.at[i, 1],
             device_id={"normal": m - 1}, device_id_type=MESH,
         )
 
-    def start_halo(i, src):
-        for copy in strike_copies(i, src):
-            copy.start()
-
+    def start_halo(i):
         @pl.when(jnp.logical_not(high))
         def _():
             up_copy(i).start()
@@ -229,10 +229,7 @@
         def _():
             down_copy(i).start()
 
-    def wait_halo(i, src):
-        for copy in strike_copies(i, src):
-            copy.wait_recv()
-
+    def wait_halo(i):
         @pl.when(jnp.logical_not(low))
         def _():
             up_copy(i).wait_recv()
@@ -241,10 +238,7 @@
         def _():
             down_copy(i).wait_recv()
 
-    def finish_halo(i, src):
-        for copy in strike_copies(i, src):
-            copy.wait_send()
-
+    def finish_halo(i):
         @pl.when(jnp.logical_not(high))
         def _():
             up_copy(i).wait_send()
@@ -253,25 +247,17 @@
         def _():
             down_copy(i).wait_send()
 
-    def set_faces(i, src):
-        faces[i, 0] = src[:, 1 : OWN + 1, 0, :]
-        faces[i, 1] = src[:, 1 : OWN + 1, 7, :]
-
-    aux = [
+    def set_faces(i, src, first):
+        faces[i, 0] = src[:, first : first + WIDE, 0, :]
+        faces[i, 1] = src[:, first : first + WIDE, 7, :]
+
+    marks_around = [
         pltpu.make_async_remote_copy(
-            mods.at[OWN], mods.at[0], aux_s.at[0], aux_r.at[0],
+            contacts.at[pl.ds(OWN, 8)], contacts.at[pl.ds(0, 8)], aux_s.at[6], aux_r.at[6],
             device_id={"strike": right}, device_id_type=MESH,
         ),
         pltpu.make_async_remote_copy(
-            mods.at[1], mods.at[OWN + 1], aux_s.at[1], aux_r.at[1],
-            device_id={"strike": left}, device_id_type=MESH,
-        ),
-        pltpu.make_async_remote_copy(
-            contacts.at[pl.ds(OWN, 8)], contacts.at[pl.ds(0, 8)], aux_s.at[2], aux_r.at[2],
-            device_id={"strike": right}, device_id_type=MESH,
-        ),
-        pltpu.make_async_remote_copy(
-            contacts.at[pl.ds(8, 8)], contacts.at[pl.ds(OWN + 8, 8)], aux_s.at[3], aux_r.at[3],
+            contacts.at[pl.ds(8, 8)], contacts.at[pl.ds(OWN + 8, 8)], aux_s.at[7], aux_r.at[7],
             device_id={"strike": left}, device_id_type=MESH,
         ),
     ]
@@ -331,7 +317,7 @@
 
     def past_copy(who):
         return pltpu.make_async_remote_copy(
-            past.at[0], past.at[1], aux_s.at[4], aux_r.at[4],
+            past.at[0], past.at[1], aux_s.at[8], aux_r.at[8],
             device_id={"strike": who}, device_id_type=MESH,
         )
 
@@ -348,7 +334,6 @@
             copy.wait_send()
 
     loads[0].wait()
-    set_faces(0, us0)
     loads[1].wait()
 
     @pl.when(plane)
@@ -356,31 +341,47 @@
         for jh in range(2):
             rows = []
             for c in range(3):
-                part = pl.ds(16 * jh, 16)
-                rows.append(jnp.where(high, faces[0, 1, c, part], faces[0, 0, c, part]))
+                a = 3 + 16 * jh
+                rows.append(jnp.where(high, us0[c, a : a + 16, 7, :], us0[c, a : a + 16, 0, :]))
             rows.append(jnp.zeros((16, 128), F32))
             block = jnp.concatenate(rows, axis=0)
             halves = [mm_nt(pack[dd], block) for dd in range(2)]
             wide[:, :, jh, :] = jnp.concatenate(halves, axis=1).reshape(NZ, GROUP, 128)
         p1[...] = wide[...].reshape(NX, YH, NZ, 2, 128).astype(BF16)
 
+    def prepare():
+        loads[2].wait()
+        loads[3].wait()
+        loads[4].wait()
+        marks = mm(flags[...].reshape(64, 32).astype(F32), widen[...]).reshape(8, 1, 8, 128)
+        scale = 1.0 - 0.5 * marks
+        mods[2 : OWN + 2] = (stiff[...].reshape(8, 4, 8, 128) * scale).reshape(OWN, 8, 128)
+        loads[5].wait()
+        contacts[8 : OWN + 8] = marked[...].astype(F32)
+        loads[6].wait()
+
+    @pl.when(feeder)
+    def _():
+        pl.semaphore_wait(barrier, 3 + NX)
+        start_all(gather_sends(0))
+
+    @pl.when(plane)
+    def _():
+        start_all(past_loads)
+
     @pl.when(low)
     def _():
         for i in range(SUB):
-            sides[i, 0] = jnp.zeros((3, OWN, 128), F32)
+            sides[i, 0] = jnp.zeros((3, WIDE, 128), F32)
 
     @pl.when(high)
     def _():
         for i in range(SUB):
-            sides[i, 1] = jnp.zeros((3, OWN, 128), F32)
-
-    loads[2].wait()
-    loads[3].wait()
-    loads[4].wait()
-    marks = mm(flags[...].reshape(64, 32).astype(F32), widen[...]).reshape(8, 1, 8, 128)
-    mods[1 : OWN + 1] = (stiff[...].reshape(8, 4, 8, 128) * (1.0 - 0.5 * marks)).reshape(OWN, 8, 128)
-    loads[5].wait()
-    contacts[8 : OWN + 8] = marked[...].astype(F32)
+            sides[i, 1] = jnp.zeros((3, WIDE, 128), F32)
+
+    us2[:, 0] = jnp.zeros((3, 8, 128), F32)
+    us2[:, WIDE - 1] = jnp.zeros((3, 8, 128), F32)
+    prepare()
 
     @pl.when(owner)
     def _():
@@ -388,18 +389,12 @@
         start_all(gather_sends(1))
         gather_self().start()
 
-    @pl.when(feeder)
-    def _():
-        pl.semaphore_wait(barrier, 3 + NX)
-        start_all(gather_sends(0))
-
     @pl.when(jnp.logical_not(plane))
     def _():
         pl.semaphore_wait(barrier, 4)
 
-    start_halo(0, us0)
-    for copy in aux:
-        copy.start()
+    start_all(strike_copies())
+    start_all(marks_around)
 
     @pl.when(plane)
     def _():
@@ -417,18 +412,28 @@
     def _():
         past_copy(s - NZ * NX).start()
 
-    def substep(i, src, dst, offset):
+    def substep(i, src, base, dst, first, count):
         for c in range(3):
-            here = src[c, 1 : OWN + 1]
+            a, b = first + base, first + count + base
+            here = src[c, a:b]
             layer = lax.broadcasted_iota(jnp.int32, here.shape, 1)
-            below = jnp.where(layer == 0, sides[i, 0, c][:, None, :], pltpu.roll(here, 1, 1))
-            above = jnp.where(layer == 7, sides[i, 1, c][:, None, :], pltpu.roll(here, 7, 1))
+            under = sides[i, 0, c, first : first + count]
+            over = sides[i, 1, c, first : first + count]
+            below = jnp.where(layer == 0, under[:, None, :], pltpu.roll(here, 1, 1))
+            above = jnp.where(layer == 7, over[:, None, :], pltpu.roll(here, 7, 1))
             lap = (
-                src[c, 2 : OWN + 2] + src[c, 0:OWN] + (above + below) + dip_sides(here) - 6.0 * here
+                src[c, a + 1 : b + 1] + src[c, a - 1 : b - 1]
+                + (above + below) + dip_sides(here) - 6.0 * here
             )
-            speed = vs[c] + time_step * (mods[1 : OWN + 1] * lap)
-            vs[c] = speed
-            dst[c, offset : offset + OWN] = here + time_step * speed
+            rows = slice(first, first + count)
+            speed = (vx if i == 0 else vy)[c, rows] + time_step * (mods[rows] * lap)
+            moved = here + time_step * speed
+            if dst is uf:
+                vs[c] = speed
+                uf[c] = moved
+            else:
+                vy[c, rows] = speed
+                dst[c, rows] = moved
 
     @pl.when(owner)
     def _():
@@ -437,14 +442,15 @@
         start_all(turn_sends())
         turn_self().start()
 
-    loads[6].wait()
-    wait_halo(0, us0)
-    substep(0, us0, us1, 1)
-    set_faces(1, us1)
-    start_halo(1, us1)
-
+    recv_all(strike_copies())
+    set_faces(0, us0, 1)
+    start_halo(0)
     for load in loads[7:]:
         load.wait()
+    wait_halo(0)
+    substep(0, us0, 1, us1, 0, WIDE)
+    set_faces(1, us1, 0)
+    start_halo(1)
 
     @pl.when(owner)
     def _():
@@ -453,51 +459,70 @@
         recv_all(turn_sends())
         turn_self().wait()
         past_copy(s ^ 1).wait_recv()
-        for h in range(YH):
-            wide[...] = r1[:, :, h].astype(F32)
-            got = jnp.concatenate(
-                [wide[:, :, jh, :].reshape(SLABS, 128) for jh in range(2)], axis=0
-            )
-            y = mm(got.T, forward[...])
-            re, im = y[:, :128], y[:, 128:]
-            tr, ti = twiddle[0], twiddle[1]
-            turned = jnp.concatenate([re * tr - im * ti, re * ti + im * tr], axis=0)
-            modes = mm(inner[...], turned)
+        pairs = range(YH)
+        spread[...] = r1[...].astype(F32)
+        got = jnp.concatenate(
+            [
+                jnp.concatenate(
+                    [spread[:, :, h, jh, :].reshape(SLABS, 128) for jh in range(2)], axis=0
+                )
+                for h in pairs
+            ],
+            axis=1,
+        )
+        y = mm(got.T, forward[...])
+        tr, ti = twiddle[0], twiddle[1]
+        turned = []
+        for h in pairs:
+            re, im = y[128 * h : 128 * h + 128, :128], y[128 * h : 128 * h + 128, 128:]
+            turned.append(jnp.concatenate([re * tr - im * ti, re * ti + im * tr], axis=0))
+        modes = mm(inner[...], jnp.concatenate(turned, axis=1))
+        forces = []
+        for h in pairs:
             older = jnp.concatenate(
                 [past[h, q, c, :, dd, :] for q in range(2) for c in range(3) for dd in range(2)],
                 axis=0,
             )
-            back = mm(outer[...], newest * modes + older)
-            re, im = back[:128], back[128:]
-            tr, ti = twiddle[2], twiddle[3]
-            turned = jnp.concatenate([re * tr - im * ti, re * ti + im * tr], axis=1)
-            pulled = mm_nt(inverse[...], turned)
+            forces.append(newest * modes[:, 128 * h : 128 * h + 128] + older)
+        back = mm(outer[...], jnp.concatenate(forces, axis=1))
+        tr, ti = twiddle[2], twiddle[3]
+        turned = []
+        for h in pairs:
+            re, im = back[:128, 128 * h : 128 * h + 128], back[128:, 128 * h : 128 * h + 128]
+            turned.append(jnp.concatenate([re * tr - im * ti, re * ti + im * tr], axis=1))
+        pulled = mm_nt(inverse[...], jnp.concatenate(turned, axis=0))
+        for h in pairs:
             for jh in range(2):
-                wide[:, :, jh, :] = pulled[64 * jh : 64 * jh + 64].reshape(NZ, GROUP, 128)
-            p2[:, :, h] = wide[...].astype(BF16)
+                block = pulled[64 * jh : 64 * jh + 64, 128 * h : 128 * h + 128]
+                spread[:, :, h, jh, :] = block.reshape(NZ, GROUP, 128)
+        p2[...] = spread[...].astype(BF16)
         start_all(return_sends())
         return_self().start()
+
+    wait_halo(1)
+    substep(1, us1, 0, us2, 1, WIDE - 2)
+    set_faces(2, us2, 0)
+    start_halo(2)
+
+    @pl.when(owner)
+    def _():
         recv_all(return_sends())
         return_self().wait()
         start_all(scatter_sends())
         scatter_self().start()
 
-    wait_halo(1, us1)
-    substep(1, us1, us2, 1)
-    set_faces(2, us2)
-    start_halo(2, us2)
-
-    wait_halo(2, us2)
-    substep(2, us2, uf, 0)
-    for copy in aux:
-        copy.wait_recv()
+    wait_halo(2)
+    substep(2, us2, 0, uf, 2, OWN)
+    recv_all(marks_around)
 
     @pl.when(plane)
     def _():
         mod2[...] = jnp.zeros_like(mod2)
         pulls[...] = jnp.zeros_like(pulls)
         for k in range(3):
-            mod2[k, 7:41] = jnp.where(high, mods[:, 7 - k, :], mods[:, k, :])
+            mod2[k, 7:41] = jnp.where(
+                high, mods[1 : OWN + 3, 7 - k, :], mods[1 : OWN + 3, k, :]
+            )
 
     @pl.when(owner)
     def _():
@@ -511,15 +536,25 @@
     @pl.when(plane)
     def _():
         wide[...] = q2[...].astype(F32).reshape(NZ, GROUP, 2, 128)
-        pieces = []
-        for jh in range(2):
-            turned = wide[:, :, jh, :].reshape(SLABS, 128).T
-            pieces.append(mm(turned[:64], unpack[0]) + mm(turned[64:], unpack[1]))
+        turned = jnp.concatenate(
+            [wide[:, :, jh, :].reshape(SLABS, 128) for jh in range(2)], axis=1
+        ).T
+        pieces = sum(
+            mm(
+                jnp.concatenate(
+                    [turned[64 * dd : 64 * dd + 64], turned[128 + 64 * dd : 192 + 64 * dd]], axis=0
+                ),
+                unpack[dd],
+            )
+            for dd in range(2)
+        )
+        pieces = [pieces[:64], pieces[64:]]
 
         def lap2(x):
             return pltpu.roll(x, 1, 0) + pltpu.roll(x, 47, 0) + dip_sides(x) - 6.0 * x
 
         half = time_step
+        responses = []
         for c in range(3):
             a = 16 * c
             pulls[c, 6:8] = pieces[0][48 + 2 * c : 50 + 2 * c]
@@ -537,17 +572,25 @@
                 half * (mod2[2] * u1),
             )
             u0, u1, u2 = u0 + half * v0, u1 + half * v1, half * v2
-            force[c, 0] = u0[8:40]
-            force[c, 1] = u1[8:40]
-            force[c, 2] = u2[8:40]
-            force[c, 3] = v0[8:40]
-            force[c, 4] = v1[8:40]
-            force[c, 5] = v2[8:40]
-
-    for i, src in enumerate((us0, us1, us2)):
-        finish_halo(i, src)
-    for copy in aux:
-        copy.wait_send()
+            responses.append([x[8:40] for x in (u0, u1, u2, v0, v1, v2)])
+
+        @pl.when(low)
+        def _():
+            for c in range(3):
+                for k in range(3):
+                    uf[c, :, k, :] = uf[c, :, k, :] + responses[c][k]
+                    vs[c, :, k, :] = vs[c, :, k, :] + responses[c][3 + k]
+
+        @pl.when(high)
+        def _():
+            for c in range(3):
+                for k in range(3):
+                    uf[c, :, 7 - k, :] = uf[c, :, 7 - k, :] + responses[c][k]
+                    vs[c, :, 7 - k, :] = vs[c, :, 7 - k, :] + responses[c][3 + k]
+
+    for i in range(SUB):
+        finish_halo(i)
+    sent_all(strike_copies() + marks_around)
 
     @pl.when(owner)
     def _():
@@ -559,55 +602,29 @@
         past_copy(s - NZ * NX).wait_send()
 
 
-def finish(uf, vs, force, u_out, v_out, u_new, v_new, sem):
-    m = lax.axis_index("normal")
-    low, high = m == 0, m == 7
-    plane = jnp.logical_or(low, high)
-
-    def store(a, b):
-        copies = [
-            pltpu.make_async_copy(a, u_out, sem.at[0]),
-            pltpu.make_async_copy(b, v_out, sem.at[1]),
-        ]
-        for copy in copies:
-            copy.start()
-        for copy in copies:
-            copy.wait()
-
-    @pl.when(jnp.logical_not(plane))
-    def _():
-        store(uf, vs)
-
-    @pl.when(plane)
-    def _():
-        u_new[...] = uf[...]
-        v_new[...] = vs[...]
-
-        @pl.when(low)
-        def _():
-            for k in range(3):
-                u_new[:, :, k, :] = uf[:, :, k, :] + force[:, k]
-                v_new[:, :, k, :] = vs[:, :, k, :] + force[:, 3 + k]
-
-        @pl.when(high)
-        def _():
-            for k in range(3):
-                u_new[:, :, 7 - k, :] = uf[:, :, 7 - k, :] + force[:, k]
-                v_new[:, :, 7 - k, :] = vs[:, :, 7 - k, :] + force[:, 3 + k]
-
-        store(u_new, v_new)
+def finish(uf, vs, u_out, v_out, sem):
+    copies = [
+        pltpu.make_async_copy(uf, u_out, sem.at[0]),
+        pltpu.make_async_copy(vs, v_out, sem.at[1]),
+    ]
+    for copy in copies:
+        copy.start()
+    for copy in copies:
+        copy.wait()
 
 
 def body(displacement, velocity, stiffness, yield_flags, contact, history, kern):
     any_space = pl.BlockSpec(memory_space=pl.ANY)
     dma, vmem = pltpu.SemaphoreType.DMA, pltpu.VMEM
     scratch = [
-        vmem((3, OWN + 2, 8, 128), F32),
-        vmem((3, OWN + 2, 8, 128), F32),
-        vmem((3, OWN + 2, 8, 128), F32),
+        vmem((3, OWN + 6, 8, 128), F32),
+        vmem((3, WIDE, 8, 128), F32),
+        vmem((3, WIDE, 8, 128), F32),
+        vmem((3, WIDE, 8, 128), F32),
+        vmem((3, WIDE, 8, 128), F32),
         vmem((OWN, 8, 128), F32),
         vmem((8, 8, 32), jnp.int32),
-        vmem((OWN + 2, 8, 128), F32),
+        vmem((WIDE, 8, 128), F32),
         vmem((OWN, 128), jnp.int32),
         vmem((OWN + 16, 128), F32),
         vmem((N2, 7, 2, 3, 2, 128), BF16),
@@ -621,8 +638,8 @@
         vmem((2, 64, 128), BF16),
         vmem((32, 128), BF16),
         vmem((4, 128, 128), F32),
-        vmem((SUB, 2, 3, OWN, 128), F32),
-        vmem((SUB, 2, 3, OWN, 128), F32),
+        vmem((SUB, 2, 3, WIDE, 128), F32),
+        vmem((SUB, 2, 3, WIDE, 128), F32),
         vmem((NX, YH, NZ, 2, 128), BF16),
         vmem((GROUP, YH, NZ, 2, 128), BF16),
         vmem((NZ, GROUP, YH, 2, 128), BF16),
@@ -630,15 +647,16 @@
         vmem((NZ, GROUP, YH, 2, 128), BF16),
         vmem((NX, NZ, YH, 2, 128), BF16),
         vmem((NZ, GROUP, 2, 128), F32),
+        vmem((NZ, GROUP, YH, 2, 128), F32),
         vmem((3, OWN + 16, 128), F32),
         vmem((3, OWN + 16, 128), F32),
         dma((13,)),
         dma((2, N2)),
         dma((4,)),
-        dma((SUB, 4)),
-        dma((SUB, 4)),
-        dma((5,)),
-        dma((5,)),
+        dma((SUB, 2)),
+        dma((SUB, 2)),
+        dma((9,)),
+        dma((9,)),
         dma((4, 8)),
         dma((4, 8)),
     ]
@@ -647,9 +665,9 @@
     fix = lambda x: pltpu.with_memory_space_constraint(x, pltpu.HBM)
     pieces = pl.pallas_call(
         kernel,
-        out_shape=(out, out, jax.ShapeDtypeStruct((3, 6, OWN, 128), F32)),
+        out_shape=(out, out),
         in_specs=[any_space] * 15,
-        out_specs=(in_vmem,) * 3,
+        out_specs=(in_vmem,) * 2,
         scratch_shapes=scratch,
         compiler_params=pltpu.CompilerParams(
             collective_id=0, has_side_effects=True, vmem_limit_bytes=GRANT
@@ -662,9 +680,9 @@
     return pl.pallas_call(
         finish,
         out_shape=(out, out),
-        in_specs=[in_vmem] * 3,
+        in_specs=[in_vmem] * 2,
         out_specs=(any_space, any_space),
-        scratch_shapes=[vmem(out.shape, F32), vmem(out.shape, F32), dma((2,))],
+        scratch_shapes=[dma((2,))],
         compiler_params=pltpu.CompilerParams(vmem_limit_bytes=GRANT),
         name="slab_finish",
     )(*pieces)

time: 39.3 us -> 38.2 us (0.972)
  Pallas kernels: 38.6 us -> 37.4 us
    pallas_call x2, Pallas kernels: 38.6 us -> 37.4 us  [the longest x1 36.5 us: body(): pl.pallas_call(kernel, out_shape=(out, out), in_specs=[any_space] * 15, o...]
where the time goes in v4:
time: 38.2 us; the launch traced here: 38 us
  Pallas kernels  37.4 us (98%)
  between operations  0.64 us (2%)
    pallas_call x1, Pallas kernels, body(): pl.pallas_call(kernel, out_shape=(out, out), in_specs=[any_space] * 15, o...  36.5 us
    pallas_call x1, Pallas kernels, body(): pl.pallas_call(finish, out_shape=(out, out), in_specs=[in_vmem] * 2, out_...  0.89 us

profile of v4, /device:TPU:32, one launch (start us, length us, event | category | flops | bytes accessed | tf_op | source)
XLA Modules:
  0.0 38.0 jit_solution(5386960191559315622)
XLA Ops:
  0.6 36.5 %slab_step.1 = (f32[3,32,8,128]{3,2,1,0:T(8,128)S(1)}, f32[3,32,8,128]{3,2,1,0:T(8,128)S(1)}) custom-call(f32[3,32,8,128]{3,2,1,0:T(8,128)} %u_in.1, f32[3,32,8,128]{3,2,1,0:T(8,128)} %v_in.1, f32[32,8,128]{2,1,0:T(8,128)} %stiff_in.1, s32[8,8,32]{2,1,0:T(8,128)} %flags_in.1, s32[2,32,128]{2,1,0:T(8,128)} %contact_in.1, ...), custom_call_target="tpu_custom_call" | custom-call | tf_op jit(solution)/shard_map/slab_step/pallas_call | solution.py:666
  37.1 0.9 %slab_finish.1 = (f32[3,32,8,128]{3,2,1,0:T(8,128)}, f32[3,32,8,128]{3,2,1,0:T(8,128)}) custom-call(f32[3,32,8,128]{3,2,1,0:T(8,128)S(1)} %get-tuple-element.4.uf, f32[3,32,8,128]{3,2,1,0:T(8,128)S(1)} %get-tuple-element.5.vs), custom_call_target="tpu_custom_call" | custom-call | tf_op jit(solution)/shard_map/slab_finish/pallas_call | solution.py:680
